TPU v7x, 512 devices: a whole 4x8x8 slice. The times are simulated.
512 devices in a mesh: ctx: 64 (over z, y_hi, core), head: 8 (over x, y_lo).
Axes of the slice: x: 4, y: 8 (y_hi: 4, y_lo: 2; y = y_hi * 2 + y_lo), z: 8, core: 2. Of those that a mesh axis runs over, the one named last changes fastest.
Arguments:
- prompt_latent: bfloat16 [6144, 576], P('ctx'), may hold values from -8 to 8
- prefill_query: bfloat16 [4096, 64, 192], P('ctx', 'head'), may hold values from -12 to 12
- span_start: int32 [1], replicated, may hold values from 0 to 2048
- w_uk: bfloat16 [64, 128, 512], P('head'), may hold values from -0.5 to 0.5
- w_uv: bfloat16 [64, 512, 128], P('head'), may hold values from -0.25 to 0.25
- decode_latent: bfloat16 [256, 256, 576], P(None, 'ctx'), may hold values from -8 to 8
- owner_slot: int32 [256], replicated, may hold values from 0 to 255, each once
- lengths: int32 [256], P('ctx'), may hold values from 1 to 256
- hidden_new: bfloat16 [4, 256, 7168], P(None, 'ctx', 'head'), may hold values from -6 to 6
- decode_query: bfloat16 [4, 256, 64, 192], P(None, 'ctx', 'head'), may hold values from -12 to 12
- w_down: bfloat16 [7168, 576], P('head'), may hold values from -0.0625 to 0.0625
- kv_gain: float32 [512], replicated, may hold values from 0.5 to 1.5
Outputs:
- prefill_out: bfloat16 [4096, 64, 128], P('ctx', 'head')
- decode_out: bfloat16 [4, 256, 64, 128], P(None, 'ctx', 'head')
Inputs may be any that keep to these rules, and one draw needn't show every extreme that they name: span_start + 4096 <= 6144. `owner_slot`: each slot once.
All inputs are finite; a program needn't handle non-finite values.
Results may differ from a plain program's by a relative error of at most 0.014.
Values may be sent and summed in bfloat16 or wider, within the bound.
No kernel may reach another device: no remote copies, remote signals or barrier semaphores. Data moves between devices by JAX's collectives and lax.ppermute only.
A program may use at most 128 MiB of HBM per device.

v0:
```python
import jax
import jax.numpy as jnp
from jax import lax
from jax.sharding import PartitionSpec as P

KV_RANK = 512
ROPE = 64
NOPE = 128


def gathered_total(array, axis):
    return lax.all_gather(array, axis).astype(jnp.float32).sum(0)


def absorb(query, w_uk, form):
    absorbed = jnp.einsum(form, query[..., :NOPE], w_uk, preferred_element_type=jnp.float32).astype(
        jnp.bfloat16
    )
    return jnp.concatenate([absorbed, query[..., NOPE:]], axis=-1)


def body(
    prompt_latent,
    prefill_query,
    span_start,
    w_uk,
    w_uv,
    decode_latent,
    owner_slot,
    lengths,
    hidden_new,
    decode_query,
    w_down,
    kv_gain,
):
    scale = (NOPE + ROPE) ** (-0.5)
    heads_here = w_uk.shape[0]
    queries = prefill_query.shape[0]
    width = prompt_latent.shape[1]
    full_query = absorb(prefill_query, w_uk, "qhn,hnc->qhc")
    rows = full_query.reshape(queries * heads_here, width)
    first = span_start[0] + lax.axis_index("ctx") * queries
    positions = jnp.repeat(first + jnp.arange(queries, dtype=jnp.int32), heads_here)
    count = rows.shape[0]
    piece = lax.all_gather(prompt_latent, "ctx", axis=0, tiled=True)
    top = jnp.full((count,), -1e30, jnp.float32)
    scores = jnp.dot(rows, piece.T, preferred_element_type=jnp.float32) * scale
    keys = jnp.arange(piece.shape[0], dtype=jnp.int32)
    allowed = keys[None, :] <= positions[:, None]
    peak = jnp.maximum(top, jnp.max(jnp.where(allowed, scores, -1e30), axis=1))
    probs = jnp.where(allowed, jnp.exp(scores - peak[:, None]), 0.0)
    total = jnp.sum(probs, axis=1)
    acc = jnp.dot(
        probs.astype(jnp.bfloat16), piece[:, :KV_RANK], preferred_element_type=jnp.float32
    )
    top, total, acc = (peak, total, acc)
    mixed = (acc / total[:, None]).astype(jnp.bfloat16).reshape(queries, heads_here, KV_RANK)
    prefill_out = jnp.einsum(
        "qhc,hcv->qhv", mixed, w_uv, preferred_element_type=jnp.float32
    ).astype(jnp.bfloat16)
    order = jnp.argsort(owner_slot)
    by_slot = decode_latent[order]
    cache = lax.all_to_all(by_slot, "ctx", split_axis=0, concat_axis=1, tiled=True)
    steps_here, owned, model_cols = hidden_new.shape
    raw_part = jnp.dot(
        hidden_new.reshape(steps_here * owned, model_cols),
        w_down,
        preferred_element_type=jnp.float32,
    )
    raw = gathered_total(raw_part.astype(jnp.bfloat16), "head").astype(jnp.float32)
    front = raw[:, :KV_RANK]
    factor = lax.rsqrt(jnp.mean(front * front, axis=1) + 1e-06)
    normed = front * factor[:, None] * kv_gain[None, :]
    new_rows = jnp.concatenate([normed, raw[:, KV_RANK:]], axis=1).astype(jnp.bfloat16)
    new_latent = new_rows.reshape(steps_here, owned, width)
    query = absorb(decode_query, w_uk, "srhn,hnc->srhc")
    cache_scores = (
        jnp.einsum("srhc,rjc->srhj", query, cache, preferred_element_type=jnp.float32) * scale
    )
    new_scores = (
        jnp.einsum("srhc,trc->srht", query, new_latent, preferred_element_type=jnp.float32) * scale
    )
    capacity = cache.shape[1]
    cache_ok = (jnp.arange(capacity, dtype=jnp.int32)[None, :] < lengths[:, None])[None, :, None, :]
    steps_idx = jnp.arange(steps_here, dtype=jnp.int32)
    new_ok = (steps_idx[None, :] <= steps_idx[:, None])[:, None, None, :]
    peak = jnp.maximum(
        jnp.max(jnp.where(cache_ok, cache_scores, -1e30), axis=3),
        jnp.max(jnp.where(new_ok, new_scores, -1e30), axis=3),
    )
    cache_p = jnp.where(cache_ok, jnp.exp(cache_scores - peak[..., None]), 0.0)
    new_p = jnp.where(new_ok, jnp.exp(new_scores - peak[..., None]), 0.0)
    total_d = jnp.sum(cache_p, axis=3) + jnp.sum(new_p, axis=3)
    mixed_d = jnp.einsum(
        "srhj,rjc->srhc",
        cache_p.astype(jnp.bfloat16),
        cache[:, :, :KV_RANK],
        preferred_element_type=jnp.float32,
    )
    mixed_d = mixed_d + jnp.einsum(
        "srht,trc->srhc",
        new_p.astype(jnp.bfloat16),
        new_latent[:, :, :KV_RANK],
        preferred_element_type=jnp.float32,
    )
    mixed_d = (mixed_d / total_d[..., None]).astype(jnp.bfloat16)
    decode_out = jnp.einsum(
        "srhc,hcv->srhv", mixed_d, w_uv, preferred_element_type=jnp.float32
    ).astype(jnp.bfloat16)
    return (prefill_out, decode_out)


def solution(mesh):
    in_specs = (
        P("ctx", None),
        P("ctx", "head", None),
        P(),
        P("head", None, None),
        P("head", None, None),
        P(None, "ctx", None),
        P(),
        P("ctx"),
        P(None, "ctx", "head"),
        P(None, "ctx", "head", None),
        P("head", None),
        P(),
    )
    out_specs = (P("ctx", "head", None), P(None, "ctx", "head", None))
    return jax.shard_map(body, mesh=mesh, in_specs=in_specs, out_specs=out_specs, check_vma=False)
```

profile of v0, /device:TPU:1, one launch (start us, length us, event | category | flops | bytes accessed | tf_op | source)
XLA Modules:
  0.0 162.7 jit_solution(17670993804524702445)
XLA Ops:
  7.2 0.0 copy-start
  7.2 0.0 all-gather.3.cloned.1.call-start
  7.2 0.7 all-gather.3.cloned.1.call-update
  7.9 2.8 %copy.43 = bf16[256,4,576]{2,1,0:T(4,128)(2,1)S(1)} copy(bf16[256,4,576]{0,2,1:T(8,128)(2,1)} %param.17) | data formatting | bytes 2359296 | tf_op args[5]
  10.7 0.0 copy-start.1
  10.7 3.9 %sort.17 = (s32[256]{0:T(256)}, s32[256]{0:T(256)S(1)}) sort(s32[256]{0:T(256)} %param.18, s32[256]{0:T(256)S(1)} %iota.33), dimensions={0}, to_apply=%region_2.3 | sort | flops 2048 | bytes 4096 | tf_op jit(solution)/shard_map/jit(argsort)/sort | solution.py:61
  14.7 2.9 %gather_fusion = bf16[256,4,576]{2,1,0:T(4,128)(2,1)} fusion(bf16[256,4,576]{2,1,0:T(4,128)(2,1)S(1)} %copy.43, s32[1024]{0:T(1024)S(1)} %pad_clamp_fusion), kind=kCustom, calls=%fused_computation | custom fusion | bytes 2360320 | tf_op jit(solution)/shard_map/gather | solution.py:62
  17.6 17.6 %all-to-all-start = ((bf16[256,4,576]{2,1,0:T(4,128)(2,1)}), bf16[256,4,576]{2,1,0:T(4,128)(2,1)S(1)}, u32[]{:S(2)}, u32[]{:S(2)}) async-start(bf16[256,4,576]{2,1,0:T(4,128)(2,1)} %gather_fusion), calls=%async_computation | async-start | bytes 2621440 | tf_op jit(solution)/shard_map/all_to_all | solution.py:63
  35.2 1.6 slice.27
  36.8 1.6 slice.26
  38.4 1.4 slice.31
  39.7 1.4 slice.30
  41.8 0.1 broadcast_in_dim.68
  41.8 0.7 le.39
  42.5 0.9 copy.68
  43.4 1.4 copy.71
  44.8 1.4 reshape.70
  46.2 1.6 convolution_convert_fusion.4
  47.8 35.9 %all-gather = bf16[128,576]{1,0:T(8,128)(2,1)S(1)} all-gather(bf16[16,576]{1,0:T(8,128)(2,1)S(1)} %convolution_convert_fusion.4), channel_id=2, replica_groups=mesh['ctx'=64,'head'=8] {'head'}, dimensions={0}, use_global_device_ids=true | all-gather | bytes 165888 | tf_op jit(solution)/shard_map/all_gather | solution.py:12
  83.7 0.6 copy.51
  84.3 0.1 multiply_reduce_fusion
  84.4 0.8 multiply_convert_fusion
  85.2 0.6 concatenate.17
  85.8 0.0 copy-start.3
  85.8 0.8 copy.50
  86.6 0.0 copy-done
  86.6 0.0 copy-start.5
  86.6 1.0 fusion.14
  87.6 0.8 pad_maximum_fusion.1
  88.5 0.0 copy-start.2
  88.5 1.3 fusion.10
  89.8 0.9 pad_maximum_fusion
  90.8 0.7 iota_compare_fusion.1
  91.5 0.0 copy-done.5
  91.5 0.0 copy-done.2
  91.5 1.2 select_reduce_fusion.2
  92.7 0.0 all-to-all-done
  92.7 0.5 copy.44
  93.3 0.4 slice.37
  93.6 1.5 select_reduce_fusion.1
  95.2 0.8 fusion.51
  95.9 0.2 fusion.44
  96.1 0.4 fusion.24
  96.5 0.0 copy-done.3
  96.5 1.0 fusion.13
  97.5 0.0 copy-done.1
  97.5 0.3 fusion.22
  97.8 0.6 copy.56
  98.5 0.0 copy-start.4
  98.5 37.6 %all-gather.3.cloned.1.call-done = bf16[6144,576]{1,0:T(8,128)(2,1)} async-done(((bf16[96,576]{1,0:T(8,128)(2,1)}), bf16[6144,576]{1,0:T(8,128)(2,1)}) %all-gather.3.cloned.1.call-update) | async-done | bytes 7077904 | tf_op jit(solution)/shard_map/all_gather | solution.py:45
  136.0 8.4 %select_reduce_fusion = (f32[512]{0:T(512)S(1)}, f32[512,6144]{1,0:T(8,128)S(1)}) fusion(s32[512]{0:T(512)} %le.39, bf16[6144,576]{1,0:T(8,128)(2,1)} %all-gather.3.cloned.1.call-done, bf16[64,8,576]{2,0,1:T(8,128)(2,1)} %pad_maximum_fusion), kind=kOutput, calls=%fused_computation.2 | convolution fusion | flops 3636461056 | bytes 20254720 | tf_op jit(solution)/shard_map/dot_general | solution.py:47
  144.5 0.0 copy-done.4
  144.5 3.7 %fusion = f32[512]{0:T(512)S(1)} fusion(f32[512,6144]{1,0:T(8,128)S(1)} %get-tuple-element.11, f32[512]{0:T(512)S(1)} %broadcast_maximum_fusion, s32[512]{0:T(512)S(1)} %copy-done.4), kind=kLoop, calls=%fused_computation.4 | loop fusion | flops 15728128 | bytes 12589056 | tf_op jit(solution)/shard_map/reduce_sum | solution.py:52
  148.1 6.5 %fusion.31 = bf16[64,8,512]{2,1,0:T(8,128)(2,1)S(1)} fusion(bf16[6144,576]{1,0:T(8,128)(2,1)} %all-gather.3.cloned.1.call-done, f32[512,6144]{1,0:T(8,128)S(1)} %get-tuple-element.11, f32[512]{0:T(512)S(1)} %broadcast_maximum_fusion, s32[512]{0:T(512)S(1)} %copy-done.4, f32[512]{0:T(512)S(1)} %fusion), kind=kOutput, calls=%fused_computation.35 | convolution fusion | flops 3237478400 | bytes 19404800 | tf_op jit(solution)/shard_map/dot_general | solution.py:53
  154.7 0.4 fusion.15
  155.1 0.7 copy.55
  (11 shorter events, 0.1 us)
Async XLA Ops:
  7.2 79.4 %copy-start = (bf16[8,128,512]{2,1,0:T(8,128)(2,1)S(1)}, bf16[8,128,512]{2,1,0:T(8,128)(2,1)}, u32[]{:S(2)}) copy-start(bf16[8,128,512]{2,1,0:T(8,128)(2,1)} %param.15) | copy-start | bytes 3145732
  7.2 128.8 %all-gather.3.cloned.1.call-start = ((), (), s32[]{:S(2)}) async-start(), calls=%async_computation.1 | async-start | bytes 7987200 | tf_op jit(solution)/shard_map/all_gather | solution.py:45
  10.7 86.8 %copy-start.1 = (bf16[8,512,128]{2,1,0:T(8,128)(2,1)S(1)}, bf16[8,512,128]{2,1,0:T(8,128)(2,1)}, u32[]{:S(2)}) copy-start(bf16[8,512,128]{2,1,0:T(8,128)(2,1)} %param.16) | copy-start | bytes 3145732
  17.6 75.1 %all-to-all-start = ((bf16[256,4,576]{2,1,0:T(4,128)(2,1)}), bf16[256,4,576]{2,1,0:T(4,128)(2,1)S(1)}, u32[]{:S(2)}, u32[]{:S(2)}) async-start(bf16[256,4,576]{2,1,0:T(4,128)(2,1)} %gather_fusion), calls=%async_computation | async-start | bytes 2621440 | tf_op jit(solution)/shard_map/all_to_all | solution.py:63
  85.8 10.7 %copy-start.3 = (bf16[4,4,512]{2,1,0:T(4,128)(2,1)S(1)}, bf16[4,4,512]{2,1,0:T(4,128)(2,1)}, u32[]{:S(2)}) copy-start(bf16[4,4,512]{2,1,0:T(4,128)(2,1)} %concatenate.17) | copy-start | bytes 49156
  86.6 4.9 %copy-start.5 = (pred[4,4]{1,0:T(4,128)(4,1)}, pred[4,4]{1,0:T(4,128)(4,1)S(1)}, u32[]{:S(2)}) copy-start(pred[4,4]{1,0:T(4,128)(4,1)S(1)} %iota_compare_fusion.2) | copy-start | bytes 52
  88.5 3.0 %copy-start.2 = (bf16[4,4,8,576]{3,1,0,2:T(4,128)(2,1)}, bf16[4,4,8,576]{3,1,0,2:T(4,128)(2,1)S(1)}, u32[]{:S(2)}) copy-start(bf16[4,4,8,576]{3,1,0,2:T(4,128)(2,1)S(1)} %pad_maximum_fusion.1) | copy-start | bytes 442372
  98.5 46.0 %copy-start.4 = (s32[512]{0:T(512)S(1)}, s32[512]{0:T(512)}, u32[]{:S(2)}) copy-start(s32[512]{0:T(512)} %le.39) | copy-start | bytes 6148
Sparse Core Ops, SparseCore 0:
  11.3 124.6 all-gather.2
where the time goes:
time: 164 us; the launch traced here: 163 us
  waiting for transfers between devices  38.2 us (23%)
  blocking collectives  35.9 us (22%)
  matrix products  23.7 us (14%)
  local copies, waits for them, and re-layouts  20.3 us (12%)
  starting transfers between devices  17.7 us (11%)
  between operations  14.9 us (9%)
  other arithmetic  12 us (7%)
    all_gather x1, waiting for transfers between devices, body(): piece = lax.all_gather(prompt_latent, 'ctx', axis=0, tiled=True)  37.6 us
    all_gather x1, blocking collectives, gathered_total(): return lax.all_gather(array, axis).astype(jnp.float32).sum(0)  35.9 us
    all_to_all x1, starting transfers between devices, body(): lax.all_to_all(by_slot, 'ctx', split_axis=0, concat_axis=1, tiled=True)  17.6 us
    dot_general x1, matrix products, body(): scores = jnp.dot(rows, piece.T, preferred_element_type=jnp.float32) * scale  8.44 us
    dot_general x1, matrix products, body(): jnp.dot(probs.astype(jnp.bfloat16), piece[:, :KV_RANK], preferred_element...  6.52 us
    unnamed x17, local copies, waits for them, and re-layouts  6.51 us
    sort x1, other arithmetic, body(): order = jnp.argsort(owner_slot)  3.92 us
    reduce_sum x1, other arithmetic, body(): total = jnp.sum(probs, axis=1)  3.65 us
  transfers between devices with their start and end apart: 2, of which 1 were waited for; matrix products, arithmetic and copies ran while one was open for 22% of the time, Pallas kernels for 0%

commit v1 on v0

--- a/solution.py
+++ b/solution.py
@@ -42,7 +42,17 @@
     first = span_start[0] + lax.axis_index("ctx") * queries
     positions = jnp.repeat(first + jnp.arange(queries, dtype=jnp.int32), heads_here)
     count = rows.shape[0]
-    piece = lax.all_gather(prompt_latent, "ctx", axis=0, tiled=True)
+
+    def _clear_tables(xs, join_dim):
+        w1 = jnp.concatenate(
+            lax.all_to_all(
+                jnp.stack([xs for _ in range(lax.axis_size("ctx"))], axis=0), "ctx", 0, 0
+            ),
+            axis=join_dim,
+        )
+        return w1
+
+    piece = _clear_tables(prompt_latent, 0)
     top = jnp.full((count,), -1e30, jnp.float32)
     scores = jnp.dot(rows, piece.T, preferred_element_type=jnp.float32) * scale
     keys = jnp.arange(piece.shape[0], dtype=jnp.int32)

time: 164 us -> 357 us (2.18); the launches traced: 163 us -> 351 us
  blocking collectives: 35.9 us -> 286 us
  waiting for transfers between devices: 38.2 us -> 0.01 us
  between operations: 14.9 us -> 1.5 us
  starting transfers between devices: 17.7 us -> 8.82 us
    all_gather x1, blocking collectives: 35.9 us -> 228 us  [gathered_total(): return lax.all_gather(array, axis).astype(jnp.float32).sum(0)]
    all_to_all x0 -> x1, blocking collectives: none -> 58 us  [body(): lax.all_to_all(by_slot, 'ctx', split_axis=0, concat_axis=1, tiled=True)]
    all_gather x1 -> x0, waiting for transfers between devices: 37.6 us -> none  [body(): piece = lax.all_gather(prompt_latent, 'ctx', axis=0, tiled=True)]
    all_to_all x1, starting transfers between devices: 17.6 us -> 8.82 us  [_clear_tables(): lax.all_to_all(jnp.stack([xs for _ in range(lax.axis_size('ctx'))], axis=...]
    another operation x0 -> x1, local copies, waits for them, and re-layouts: none -> 4.67 us  [_clear_tables(): jnp.stack([xs for _ in range(lax.axis_size('ctx'))], axis=0)]
  transfers between devices with their start and end apart: 2 -> 1, of which waited for: 1 -> 0; matrix products, arithmetic and copies ran while one was open for 22% -> 6% of each run, Pallas kernels for 0% -> 0%
where the time goes in v1:
time: 357 us; the launch traced here: 351 us
  blocking collectives  286 us (80%)
  matrix products  22.2 us (6%)
  local copies, waits for them, and re-layouts  22.1 us (6%)
  other arithmetic  10.5 us (3%)
  starting transfers between devices  8.82 us (2%)
    all_gather x1, blocking collectives, gathered_total(): return lax.all_gather(array, axis).astype(jnp.float32).sum(0)  228 us
    all_to_all x1, blocking collectives, body(): lax.all_to_all(by_slot, 'ctx', split_axis=0, concat_axis=1, tiled=True)  58 us
    dot_general x1, matrix products, body(): scores = jnp.dot(rows, piece.T, preferred_element_type=jnp.float32) * scale  9.04 us
    all_to_all x1, starting transfers between devices, _clear_tables(): lax.all_to_all(jnp.stack([xs for _ in range(lax.axis_size('ctx'))], axis=...  8.82 us
  transfers between devices with their start and end apart: 1, of which 0 were waited for; matrix products, arithmetic and copies ran while one was open for 6% of the time, Pallas kernels for 0%

profile of v1, /device:TPU:1, one launch (start us, length us, event | category | flops | bytes accessed | tf_op | source)
XLA Modules:
  0.0 351.1 jit_solution(125892703991407364)
XLA Ops:
  0.6 0.0 copy-start
  0.6 2.9 copy.43
  3.5 3.8 %sort.17 = (s32[256]{0:T(256)}, s32[256]{0:T(256)S(1)}) sort(s32[256]{0:T(256)} %param.18, s32[256]{0:T(256)S(1)} %iota.33), dimensions={0}, to_apply=%region_2.3 | sort | flops 2048 | bytes 4096 | tf_op jit(solution)/shard_map/jit(argsort)/sort | solution.py:71
  7.4 2.8 gather_fusion
  10.2 58.0 %all_to_all.23 = bf16[256,4,576]{2,1,0:T(4,128)(2,1)S(1)} all-to-all(bf16[256,4,576]{2,1,0:T(4,128)(2,1)} %gather_fusion), channel_id=1, replica_groups=mesh['ctx'=64,'head'=8] {'ctx'}, dimensions={0} | all-to-all | bytes 2359296 | tf_op jit(solution)/shard_map/all_to_all | solution.py:73
  68.2 4.7 %stack.2 = bf16[64,96,576]{2,1,0:T(8,128)(2,1)} broadcast(bf16[96,576]{1,0:T(8,128)(2,1)} %param.12), dimensions={1,2} | broadcast | bytes 7188480 | tf_op jit(solution)/shard_map/stack | solution.py:49
  72.9 0.0 copy-start.4
  72.9 0.0 copy-start.2
  72.9 0.0 copy-start.6
  72.9 8.8 %all-to-all-start = ((bf16[64,96,576]{2,1,0:T(8,128)(2,1)}), bf16[64,96,576]{2,1,0:T(8,128)(2,1)}, u32[]{:S(2)}, u32[]{:S(2)}) async-start(bf16[64,96,576]{2,1,0:T(8,128)(2,1)} %stack.2), calls=%async_computation | async-start | bytes 15728640 | tf_op jit(solution)/shard_map/all_to_all | solution.py:48
  81.7 1.6 slice.27
  83.3 1.6 slice.26
  84.9 0.0 copy-done.4
  84.9 0.6 slice.31
  85.5 0.6 slice.30
  86.8 0.1 broadcast_in_dim.68
  86.8 0.7 le.39
  87.5 0.9 copy.68
  88.4 1.4 copy.71
  89.8 1.4 reshape.76
  91.2 0.0 copy-done.2
  91.2 1.1 convolution_convert_fusion.4
  92.3 228.0 %all-gather = bf16[128,576]{1,0:T(8,128)(2,1)S(1)} all-gather(bf16[16,576]{1,0:T(8,128)(2,1)S(1)} %convolution_convert_fusion.4), channel_id=2, replica_groups=mesh['ctx'=64,'head'=8] {'head'}, dimensions={0}, use_global_device_ids=true | all-gather | bytes 165888 | tf_op jit(solution)/shard_map/all_gather | solution.py:12
  320.3 0.6 copy.51
  320.9 0.1 multiply_reduce_fusion
  321.0 0.0 copy-done.6
  321.0 0.1 multiply_convert_fusion
  321.2 0.0 copy-done
  321.2 0.0 copy-start.1
  321.2 1.1 fusion.14
  322.3 0.8 pad_maximum_fusion.1
  323.1 1.2 fusion.10
  324.3 0.9 pad_maximum_fusion
  325.3 0.7 iota_compare_fusion.1
  326.0 1.2 select_reduce_fusion.2
  327.2 0.5 copy.44
  327.8 0.0 copy-start.3
  327.8 0.4 slice.37
  328.1 0.6 select_reduce_fusion.1
  328.7 0.1 fusion.51
  328.8 0.2 fusion.44
  329.0 0.4 fusion.24
  329.5 0.3 fusion.13
  329.8 0.0 copy-done.1
  329.8 0.3 fusion.22
  330.1 0.6 copy.56
  330.7 0.0 all-to-all-done
  330.7 0.0 copy-done.3
  330.7 0.0 copy-start.5
  330.7 9.0 %select_reduce_fusion = (f32[512]{0:T(512)S(1)}, f32[512,6144]{1,0:T(8,128)S(1)}) fusion(s32[512]{0:T(512)} %le.39, bf16[6144,576]{1,0:T(8,128)(2,1)} %bitcast.3, bf16[64,8,576]{2,0,1:T(8,128)(2,1)S(1)} %copy-done.3), kind=kOutput, calls=%fused_computation.2 | convolution fusion | flops 3636461056 | bytes 20254720 | tf_op jit(solution)/shard_map/dot_general | solution.py:57
  339.8 0.0 copy-done.5
  339.8 3.7 %fusion = f32[512]{0:T(512)S(1)} fusion(f32[512,6144]{1,0:T(8,128)S(1)} %get-tuple-element.11, f32[512]{0:T(512)S(1)} %broadcast_maximum_fusion, s32[512]{0:T(512)S(1)} %copy-done.5), kind=kLoop, calls=%fused_computation.4 | loop fusion | flops 15728128 | bytes 12589056 | tf_op jit(solution)/shard_map/reduce_sum | solution.py:62
  343.4 6.5 %fusion.31 = bf16[64,8,512]{2,1,0:T(8,128)(2,1)S(1)} fusion(bf16[6144,576]{1,0:T(8,128)(2,1)} %bitcast.3, f32[512,6144]{1,0:T(8,128)S(1)} %get-tuple-element.11, f32[512]{0:T(512)S(1)} %broadcast_maximum_fusion, s32[512]{0:T(512)S(1)} %copy-done.5, f32[512]{0:T(512)S(1)} %fusion), kind=kOutput, calls=%fused_computation.35 | convolution fusion | flops 3237478400 | bytes 19404800 | tf_op jit(solution)/shard_map/dot_general | solution.py:63
  350.0 0.4 fusion.15
  350.4 0.7 copy.55
  (13 shorter events, 0.1 us)
Async XLA Ops:
  0.6 320.5 %copy-start = (bf16[8,128,512]{2,1,0:T(8,128)(2,1)S(1)}, bf16[8,128,512]{2,1,0:T(8,128)(2,1)}, u32[]{:S(2)}) copy-start(bf16[8,128,512]{2,1,0:T(8,128)(2,1)} %param.15) | copy-start | bytes 3145732
  72.9 12.0 %copy-start.4 = (bf16[4,4,8,192]{3,2,1,0:T(8,128)(2,1)S(1)}, bf16[4,4,8,192]{3,2,1,0:T(8,128)(2,1)}, u32[]{:S(2)}) copy-start(bf16[4,4,8,192]{3,2,1,0:T(8,128)(2,1)} %param.21) | copy-start | bytes 147460
  72.9 18.3 %copy-start.2 = (bf16[896,576]{0,1:T(8,128)(2,1)S(1)}, bf16[896,576]{0,1:T(8,128)(2,1)}, u32[]{:S(2)}) copy-start(bf16[896,576]{0,1:T(8,128)(2,1)} %param.22) | copy-start | bytes 3096580
  72.9 248.1 %copy-start.6 = (f32[512]{0:T(512)S(1)}, f32[512]{0:T(512)}, u32[]{:S(2)}) copy-start(f32[512]{0:T(512)} %param.23) | copy-start | bytes 6148
  72.9 257.8 %all-to-all-start = ((bf16[64,96,576]{2,1,0:T(8,128)(2,1)}), bf16[64,96,576]{2,1,0:T(8,128)(2,1)}, u32[]{:S(2)}, u32[]{:S(2)}) async-start(bf16[64,96,576]{2,1,0:T(8,128)(2,1)} %stack.2), calls=%async_computation | async-start | bytes 15728640 | tf_op jit(solution)/shard_map/all_to_all | solution.py:48
  321.2 8.6 %copy-start.1 = (bf16[8,512,128]{2,1,0:T(8,128)(2,1)S(1)}, bf16[8,512,128]{2,1,0:T(8,128)(2,1)}, u32[]{:S(2)}) copy-start(bf16[8,512,128]{2,1,0:T(8,128)(2,1)} %param.16) | copy-start | bytes 3145732
  327.8 3.0 copy-start.3
  330.7 9.1 %copy-start.5 = (s32[512]{0:T(512)S(1)}, s32[512]{0:T(512)}, u32[]{:S(2)}) copy-start(s32[512]{0:T(512)} %le.39) | copy-start | bytes 6148
